TPU v7x, 256 devices: a whole 4x4x8 slice. The times are simulated.
256 devices in a mesh: section: 32 (over z_lo, y, core), tensor: 8 (over z_hi, x).
Axes of the slice: x: 4, y: 4, z: 8 (z_hi: 2, z_lo: 4; z = z_hi * 4 + z_lo), core: 2. Of those that a mesh axis runs over, the one named last changes fastest.
Arguments:
- queries: bfloat16 [8192, 4096], P('section', 'tensor'), may hold values from -180 to 180
- memory: bfloat16 [512, 4096], P('section', 'tensor'), may hold values from -6 to 6
- key_weight: bfloat16 [65536, 4096], P('section', 'tensor'), may hold values from -0.09375 to 0.09375
- value_weight: bfloat16 [65536, 4096], P('section', 'tensor'), may hold values from -0.09375 to 0.09375
- grad_context: bfloat16 [8192, 4096], P('section', 'tensor'), may hold values from -6 to 6
- memory_lengths: int32 [4], replicated, may hold values from 64 to 128, as said below
Outputs:
- context: bfloat16 [8192, 4096], P('section', 'tensor')
- grad_queries: bfloat16 [8192, 4096], P('section', 'tensor')
- grad_memory: float32 [512, 4096], P('section', 'tensor')
Inputs may be any that keep to these rules, and one draw needn't show every extreme that they name: `memory_lengths`: one reaction in every draw has all 128 encoder tokens.
All inputs are finite; a program needn't handle non-finite values.
Results may differ from a plain program's by a relative error of at most 0.0171.
The roundings to bfloat16 on the way count: a program that leaves them out, or rounds other values in their place, can miss the bound.
Values may be sent and summed in bfloat16 or wider, within the bound.
No kernel may reach another device: no remote copies, remote signals or barrier semaphores. Data moves between devices by JAX's collectives and lax.ppermute only.
A program may use at most 64 MiB of HBM per device.

v0:
```python
import jax
import jax.numpy as jnp
from jax import lax
from jax.sharding import PartitionSpec as P

HDIM = 64


def partner(block, axis, distance):
    count = lax.axis_size(axis)
    route = []
    for low in range(count):
        high = low | 1 << distance
        if high != low and high < count:
            route += [(low, high), (high, low)]
    return lax.ppermute(block, axis, route)


def times_transposed(left, weight_rows):
    return lax.dot_general(
        left, weight_rows, (((1,), (1,)), ((), ())), preferred_element_type=jnp.float32
    )


def body(queries, memory, key_weight, value_weight, grad_context, memory_lengths):
    scale = HDIM ** (-0.5)
    parity = lax.axis_index("section") % 2
    react = memory_lengths.shape[0]
    half_react = react // 2
    head_cols = queries.shape[1]
    local_heads = head_cols // HDIM
    half_width = key_weight.shape[0]
    full_width = 2 * half_width
    half_start = parity * half_width
    full_rows = lax.all_gather(memory, "tensor", axis=1, tiled=True)
    own_cols = lax.dynamic_slice_in_dim(
        lax.all_gather(full_rows, "section", axis=0, tiled=True), half_start, half_width, 1
    )
    key_part = jnp.dot(own_cols, key_weight, preferred_element_type=jnp.float32)
    value_part = jnp.dot(own_cols, value_weight, preferred_element_type=jnp.float32)
    joined = jnp.concatenate([key_part, value_part], axis=1)
    key_all = joined[:, :head_cols]
    value_all = joined[:, head_cols:]
    half_rows = key_all.shape[0] // 2
    is_first = parity == 0
    own_key = jnp.where(is_first, key_all[:half_rows], key_all[half_rows:])
    other_key = jnp.where(is_first, key_all[half_rows:], key_all[:half_rows])
    own_value = jnp.where(is_first, value_all[:half_rows], value_all[half_rows:])
    other_value = jnp.where(is_first, value_all[half_rows:], value_all[:half_rows])
    recv_key, recv_value = partner((other_key, other_value), "section", 0)
    keys = (own_key + recv_key).astype(jnp.bfloat16)
    values = (own_value + recv_value).astype(jnp.bfloat16)
    lengths = lax.dynamic_slice_in_dim(memory_lengths, parity * half_react, half_react, 0)
    enc_len = keys.shape[0] // half_react
    dec_len = queries.shape[0] // half_react
    query_h = queries.reshape(half_react, dec_len, local_heads, HDIM)
    key_h = keys.reshape(half_react, enc_len, local_heads, HDIM)
    value_h = values.reshape(half_react, enc_len, local_heads, HDIM)
    cot_h = grad_context.reshape(half_react, dec_len, local_heads, HDIM)
    scores = (
        jnp.einsum("rqhd,rkhd->rhqk", query_h, key_h, preferred_element_type=jnp.float32) * scale
    )
    valid = jnp.arange(enc_len, dtype=jnp.int32)[None, :] < lengths[:, None]
    scores = jnp.where(valid[:, None, None, :], scores, jnp.float32(-1e30))
    top = jnp.max(scores, axis=-1, keepdims=True)
    expo = jnp.exp(scores - top)
    probs = expo / jnp.sum(expo, axis=-1, keepdims=True)
    probs_b = probs.astype(jnp.bfloat16)
    context = jnp.einsum(
        "rhqk,rkhd->rqhd", probs_b, value_h, preferred_element_type=jnp.float32
    ).astype(jnp.bfloat16)
    grad_p = jnp.einsum("rqhd,rkhd->rhqk", cot_h, value_h, preferred_element_type=jnp.float32)
    delta = jnp.sum(probs * grad_p, axis=-1, keepdims=True)
    grad_s = (probs * (grad_p - delta) * scale).astype(jnp.bfloat16)
    grad_q = jnp.einsum(
        "rhqk,rkhd->rqhd", grad_s, key_h, preferred_element_type=jnp.float32
    ).astype(jnp.bfloat16)
    key_grad = jnp.einsum(
        "rhqk,rqhd->rkhd", grad_s, query_h, preferred_element_type=jnp.float32
    ).astype(jnp.bfloat16)
    value_grad = jnp.einsum(
        "rhqk,rqhd->rkhd", probs_b, cot_h, preferred_element_type=jnp.float32
    ).astype(jnp.bfloat16)
    key_grad = key_grad.reshape(half_react * enc_len, head_cols)
    value_grad = value_grad.reshape(half_react * enc_len, head_cols)
    partner_key, partner_value = partner((key_grad, value_grad), "section", 0)
    layer_key_grad = jnp.where(
        is_first,
        jnp.concatenate([key_grad, partner_key], axis=0),
        jnp.concatenate([partner_key, key_grad], axis=0),
    )
    layer_value_grad = jnp.where(
        is_first,
        jnp.concatenate([value_grad, partner_value], axis=0),
        jnp.concatenate([partner_value, value_grad], axis=0),
    )
    block = times_transposed(layer_key_grad, key_weight) + times_transposed(
        layer_value_grad, value_weight
    )
    blank_rows = jnp.zeros((block.shape[0], full_width), jnp.float32)
    layer_total = lax.psum_scatter(
        lax.dynamic_update_slice_in_dim(blank_rows, block, half_start, 1),
        "section",
        scatter_dimension=0,
        tiled=True,
    )
    grad_memory = lax.psum_scatter(layer_total, "tensor", scatter_dimension=1, tiled=True)
    return (
        context.reshape(half_react * dec_len, head_cols),
        grad_q.reshape(half_react * dec_len, head_cols),
        grad_memory,
    )


def solution(mesh):
    placed = (
        P("section", "tensor"),
        P("section", "tensor"),
        P("section", "tensor"),
        P("section", "tensor"),
        P("section", "tensor"),
        P(),
    )
    return jax.shard_map(
        body,
        mesh=mesh,
        in_specs=placed,
        out_specs=(P("section", "tensor"), P("section", "tensor"), P("section", "tensor")),
        check_vma=False,
    )
```

profile of v0, /device:TPU:8, one launch (start us, length us, event | category | flops | bytes accessed | tf_op | source)
XLA Modules:
  0.0 410.7 jit_solution(8636467715947990893)
XLA Ops:
  7.2 48.3 %all_gather.6 = bf16[16,4096]{1,0:T(8,128)(2,1)} all-gather(bf16[16,512]{1,0:T(8,128)(2,1)} %param.7), channel_id=1, replica_groups=mesh['section'=32,'tensor'=8] {'tensor'}, dimensions={1}, use_global_device_ids=true | all-gather | bytes 147456 | tf_op jit(solution)/shard_map/all_gather | solution.py:35
  55.6 63.2 %all-gather.2.cloned.1.call-done = bf16[512,4096]{1,0:T(8,128)(2,1)} async-done(((bf16[16,4096]{1,0:T(8,128)(2,1)}), bf16[512,4096]{1,0:T(8,128)(2,1)}) %all-gather.2.cloned.1.call-update) | async-done | bytes 4194320 | tf_op jit(solution)/shard_map/all_gather | solution.py:37
  118.8 3.0 fusion.2
  121.8 1.0 slice_select_fusion
  123.0 1.2 fusion.4
  124.3 0.9 slice_select_fusion.1
  125.5 1.1 reshape.62
  126.5 2.0 copy.26
  128.6 2.1 reshape.63
  130.6 1.3 copy.33
  132.2 2.2 add_convert_fusion
  134.3 2.1 reshape.61
  136.4 2.0 copy.25
  138.4 1.9 add_convert_fusion.1
  140.3 1.3 reshape.60
  141.6 1.0 copy.28
  142.7 2.6 fusion.50
  145.3 0.8 fusion.17
  146.7 1.4 convolution_bitcast_fusion
  148.1 3.0 fusion.16
  151.1 1.2 copy.39
  152.4 0.5 collective-permute-start.2
  152.9 3.1 fusion.27
  156.0 4.2 %broadcast_in_dim.23 = f32[512,4096]{1,0:T(8,128)} broadcast(f32[]{:T(128)} %constant.34.clone.1), dimensions={} | broadcast | bytes 8388612 | tf_op jit(solution)/shard_map/broadcast_in_dim | solution.py:100
  160.3 3.4 add_dynamic-update-slice_fusion
  163.7 150.6 %reduce-scatter.3.cloned.1.call-done = f32[16,4096]{1,0:T(8,128)} async-done(((f32[512,4096]{1,0:T(8,128)}), f32[16,4096]{1,0:T(8,128)}) %reduce-scatter.3.cloned.1.call-update) | async-done | bytes 262160 | tf_op jit(solution)/shard_map/reduce_scatter | solution.py:101
  314.3 2.9 fusion.15
  317.2 1.2 copy.50
  318.5 1.0 reshape.59
  319.5 1.8 fusion.14
  321.6 1.0 reshape.58
  322.7 81.5 %reduce-scatter.5.cloned.1.call-done = f32[16,512]{1,0:T(8,128)} async-done(((f32[16,4096]{1,0:T(8,128)}), f32[16,512]{1,0:T(8,128)}) %reduce-scatter.5.cloned.1.call-update) | async-done | bytes 32784 | tf_op jit(solution)/shard_map/reduce_scatter | solution.py:107
  (39 shorter events, 1.9 us)
Async XLA Ops:
  7.2 111.6 %copy-start = (bf16[2048,512]{1,0:T(8,128)(2,1)S(1)}, bf16[2048,512]{1,0:T(8,128)(2,1)}, u32[]{:S(2)}) copy-start(bf16[2048,512]{1,0:T(8,128)(2,1)} %param.8) | copy-start | bytes 6291460
  7.2 111.6 %all-gather.2.cloned.1.call-start = ((), (), s32[]{:S(2)}) async-start(), calls=%async_computation.2 | async-start | bytes 4325376 | tf_op jit(solution)/shard_map/all_gather | solution.py:37
  55.6 258.7 %reduce-scatter.3.cloned.1.call-start = ((), (), s32[]{:S(2)}) async-start(), calls=%async_computation.3 | async-start | bytes 8650752 | tf_op jit(solution)/shard_map/reduce_scatter | solution.py:101
  118.8 4.2 %copy-start.2 = (bf16[2048,512]{1,0:T(8,128)(2,1)S(1)}, bf16[2048,512]{1,0:T(8,128)(2,1)}, u32[]{:S(2)}) copy-start(bf16[2048,512]{1,0:T(8,128)(2,1)} %param.9) | copy-start | bytes 6291460
  118.8 4.2 %copy-start.8 = (bf16[512,4096]{1,0:T(8,128)(2,1)S(1)}, bf16[512,4096]{1,0:T(8,128)(2,1)}, u32[]{:S(2)}) copy-start(bf16[512,4096]{1,0:T(8,128)(2,1)} %all-gather.2.cloned.1.call-done) | copy-start | bytes 12582916
  121.8 2.5 copy-start.1
  122.8 2.7 copy-start.4
  122.8 9.4 %collective-permute-start.1 = (f32[256,512]{1,0:T(8,128)}, f32[256,512]{1,0:T(8,128)}, u32[]{:S(2)}, u32[]{:S(2)}) collective-permute-start(f32[256,512]{1,0:T(8,128)} %slice_select_fusion), channel_id=1, source_target_pairs={{0,8},{8,0},{16,24},{24,16},{32,40},{40,32},{48,56},{56,48},{64,72... | collective-permute-start | bytes 1572872 | tf_op jit(solution)/shard_map/ppermute | solution.py:16
  124.3 7.7 %copy-start.9 = (s32[4]{0:T(128)S(1)}, s32[4]{0:T(128)}, u32[]{:S(2)}) copy-start(s32[4]{0:T(128)} %param.11) | copy-start | bytes 52
  125.2 13.3 %collective-permute-start = (f32[256,512]{1,0:T(8,128)}, f32[256,512]{1,0:T(8,128)}, u32[]{:S(2)}, u32[]{:S(2)}) collective-permute-start(f32[256,512]{1,0:T(8,128)} %slice_select_fusion.1), channel_id=1, source_target_pairs={{0,8},{8,0},{16,24},{24,16},{32,40},{40,32},{48,56},{56,48},{64,72... | collective-permute-start | bytes 1572872 | tf_op jit(solution)/shard_map/ppermute | solution.py:16
  132.0 13.3 %copy-start.3 = (bf16[2,128,8,64]{1,3,2,0:T(8,128)(2,1)}, bf16[2,128,8,64]{1,3,2,0:T(8,128)(2,1)S(1)}, u32[]{:S(2)}) copy-start(bf16[2,128,8,64]{1,3,2,0:T(8,128)(2,1)S(1)} %copy.33) | copy-start | bytes 786436
  140.3 5.0 %copy-start.5 = (bf16[2,128,8,64]{1,3,2,0:T(8,128)(2,1)S(1)}, bf16[2,128,8,64]{1,3,2,0:T(8,128)(2,1)}, u32[]{:S(2)}) copy-start(bf16[2,128,8,64]{1,3,2,0:T(8,128)(2,1)} %copy.26) | copy-start | bytes 786436
  140.3 5.0 %copy-start.6 = (bf16[2,128,8,64]{1,3,2,0:T(8,128)(2,1)S(1)}, bf16[2,128,8,64]{1,3,2,0:T(8,128)(2,1)}, u32[]{:S(2)}) copy-start(bf16[2,128,8,64]{1,3,2,0:T(8,128)(2,1)} %copy.25) | copy-start | bytes 786436
  146.4 6.5 %collective-permute-start.3 = (bf16[256,512]{0,1:T(8,128)(2,1)S(1)}, bf16[256,512]{0,1:T(8,128)(2,1)}, u32[]{:S(2)}, u32[]{:S(2)}) collective-permute-start(bf16[256,512]{0,1:T(8,128)(2,1)S(1)} %bitcast.62), channel_id=1, source_target_pairs={{0,8},{8,0},{16,24},{24,16},{32,40},{40,32},{48,56},{56,48},{64,72... | collective-permute-start | bytes 786440 | tf_op jit(solution)/shard_map/ppermute | solution.py:16
  152.4 3.6 collective-permute-start.2
  163.6 150.7 %copy-start.7 = (bf16[2,128,8,64]{1,3,2,0:T(8,128)(2,1)S(1)}, bf16[2,128,8,64]{1,3,2,0:T(8,128)(2,1)}, u32[]{:S(2)}) copy-start(bf16[2,128,8,64]{1,3,2,0:T(8,128)(2,1)} %copy.25) | copy-start | bytes 786436
  163.7 240.5 %reduce-scatter.5.cloned.1.call-start = ((), (), s32[]{:S(2)}) async-start(), calls=%async_computation.4 | async-start | bytes 294912 | tf_op jit(solution)/shard_map/reduce_scatter | solution.py:107
Sparse Core Ops, SparseCore 0:
  55.7 63.0 all-gather.1
  163.8 150.4 reduce-scatter.2
  318.7 85.4 reduce-scatter.4
where the time goes:
time: 411 us
  waiting for transfers between devices  295 us (72%)
  blocking collectives  48.3 us (12%)
  matrix products  23.2 us (6%)
  local copies, waits for them, and re-layouts  22.5 us (5%)
  between operations  13.9 us (3%)
  other arithmetic  5.97 us (1%)
    reduce_scatter x1, waiting for transfers between devices, body(): lax.psum_scatter(lax.dynamic_update_slice_in_dim(blank_rows, block, half_...  151 us
    reduce_scatter x1, waiting for transfers between devices, body(): lax.psum_scatter(layer_total, 'tensor', scatter_dimension=1, tiled=True)  81.5 us
    all_gather x1, waiting for transfers between devices, body(): lax.all_gather(full_rows, 'section', axis=0, tiled=True)  63.2 us
    all_gather x1, blocking collectives, body(): full_rows = lax.all_gather(memory, 'tensor', axis=1, tiled=True)  48.3 us
  transfers between devices with their start and end apart: 7, of which 3 were waited for; matrix products, arithmetic and copies ran while one was open for 8% of the time, Pallas kernels for 0%

commit v1 on v0

--- a/solution.py
+++ b/solution.py
@@ -1,9 +1,23 @@
+import functools
 import jax
 import jax.numpy as jnp
 from jax import lax
 from jax.sharding import PartitionSpec as P
 
 HDIM = 64
+
+
+def turn_block(own_rows, dev_axis):
+    clean = jnp.concatenate(
+        lax.all_to_all(
+            jnp.stack(lax.psum(1, dev_axis) * [own_rows], 0), dev_axis, split_axis=0, concat_axis=0
+        ),
+        1,
+    )
+    return clean
+
+
+_find_terms = functools.partial(turn_block, dev_axis="tensor")
 
 
 def partner(block, axis, distance):
@@ -32,7 +46,7 @@
     half_width = key_weight.shape[0]
     full_width = 2 * half_width
     half_start = parity * half_width
-    full_rows = lax.all_gather(memory, "tensor", axis=1, tiled=True)
+    full_rows = _find_terms(memory)
     own_cols = lax.dynamic_slice_in_dim(
         lax.all_gather(full_rows, "section", axis=0, tiled=True), half_start, half_width, 1
     )

time: 411 us -> 381 us (0.927)
  blocking collectives: 48.3 us -> 21.2 us
    all_gather x1 -> x0, blocking collectives: 48.3 us -> none  [body(): full_rows = lax.all_gather(memory, 'tensor', axis=1, tiled=True)]
    all_to_all x0 -> x1, blocking collectives: none -> 21.2 us  [turn_block(): lax.all_to_all(jnp.stack(lax.psum(1, dev_axis) * [own_rows], 0), dev_axis...]
    all_gather x1, waiting for transfers between devices: 63.2 us -> 58.4 us  [body(): lax.all_gather(full_rows, 'section', axis=0, tiled=True)]
where the time goes in v1:
time: 381 us; the launch traced here: 380 us
  waiting for transfers between devices  291 us (76%)
  local copies, waits for them, and re-layouts  24 us (6%)
  matrix products  23.2 us (6%)
  blocking collectives  21.2 us (6%)
  between operations  13.9 us (4%)
  other arithmetic  5.97 us (2%)
    reduce_scatter x1, waiting for transfers between devices, body(): lax.psum_scatter(lax.dynamic_update_slice_in_dim(blank_rows, block, half_...  151 us
    reduce_scatter x1, waiting for transfers between devices, body(): lax.psum_scatter(layer_total, 'tensor', scatter_dimension=1, tiled=True)  81.1 us
    all_gather x1, waiting for transfers between devices, body(): lax.all_gather(full_rows, 'section', axis=0, tiled=True)  58.4 us
    all_to_all x1, blocking collectives, turn_block(): lax.all_to_all(jnp.stack(lax.psum(1, dev_axis) * [own_rows], 0), dev_axis...  21.2 us
  transfers between devices with their start and end apart: 7, of which 3 were waited for; matrix products, arithmetic and copies ran while one was open for 8% of the time, Pallas kernels for 0%

profile of v1, /device:TPU:8, one launch (start us, length us, event | category | flops | bytes accessed | tf_op | source)
XLA Modules:
  0.0 380.3 jit_solution(13283717167567610874)
XLA Ops:
  7.2 0.9 stack.2
  8.1 21.2 %all_to_all.5 = bf16[8,16,512]{2,1,0:T(8,128)(2,1)S(1)} all-to-all(bf16[8,16,512]{2,1,0:T(8,128)(2,1)S(1)} %stack.2), channel_id=1, replica_groups=mesh['section'=32,'tensor'=8] {'tensor'}, dimensions={0} | all-to-all | bytes 262144 | tf_op jit(solution)/shard_map/all_to_all | solution.py:12
  30.1 58.4 %all-gather.2.cloned.1.call-done = bf16[512,4096]{1,0:T(8,128)(2,1)} async-done(((bf16[16,4096]{1,0:T(8,128)(2,1)}), bf16[512,4096]{1,0:T(8,128)(2,1)}) %all-gather.2.cloned.1.call-update) | async-done | bytes 4194320 | tf_op jit(solution)/shard_map/all_gather | solution.py:51
  88.5 3.0 fusion.2
  91.5 1.0 slice_select_fusion
  92.7 1.2 fusion.4
  94.0 0.9 slice_select_fusion.1
  95.1 1.1 reshape.72
  96.2 2.0 copy.50
  98.2 2.1 reshape.73
  100.3 1.3 copy.57
  101.8 2.2 add_convert_fusion
  104.0 2.1 reshape.71
  106.1 2.0 copy.49
  108.1 1.9 add_convert_fusion.1
  110.0 1.3 reshape.70
  111.3 1.0 copy.52
  112.3 2.6 fusion.50
  115.0 0.8 fusion.17
  116.4 1.4 convolution_bitcast_fusion
  117.8 3.0 fusion.16
  120.8 1.2 copy.63
  122.6 3.1 fusion.27
  125.7 4.2 %broadcast_in_dim.23 = f32[512,4096]{1,0:T(8,128)} broadcast(f32[]{:T(128)} %constant.34.clone.1), dimensions={} | broadcast | bytes 8388612 | tf_op jit(solution)/shard_map/broadcast_in_dim | solution.py:114
  130.0 3.4 add_dynamic-update-slice_fusion
  133.4 151.0 %reduce-scatter.3.cloned.1.call-done = f32[16,4096]{1,0:T(8,128)} async-done(((f32[512,4096]{1,0:T(8,128)}), f32[16,4096]{1,0:T(8,128)}) %reduce-scatter.3.cloned.1.call-update) | async-done | bytes 262160 | tf_op jit(solution)/shard_map/reduce_scatter | solution.py:115
  284.4 2.9 fusion.15
  287.3 1.2 copy.74
  288.5 1.0 reshape.69
  289.6 1.8 fusion.14
  291.7 1.0 reshape.68
  292.7 81.1 %reduce-scatter.5.cloned.1.call-done = f32[16,512]{1,0:T(8,128)} async-done(((f32[16,4096]{1,0:T(8,128)}), f32[16,512]{1,0:T(8,128)}) %reduce-scatter.5.cloned.1.call-update) | async-done | bytes 32784 | tf_op jit(solution)/shard_map/reduce_scatter | solution.py:121
  (41 shorter events, 3.1 us)
Async XLA Ops:
  7.2 81.3 %copy-start = (bf16[2048,512]{1,0:T(8,128)(2,1)S(1)}, bf16[2048,512]{1,0:T(8,128)(2,1)}, u32[]{:S(2)}) copy-start(bf16[2048,512]{1,0:T(8,128)(2,1)} %param.8) | copy-start | bytes 6291460
  7.2 81.3 %all-gather.2.cloned.1.call-start = ((), (), s32[]{:S(2)}) async-start(), calls=%async_computation.3 | async-start | bytes 4325376 | tf_op jit(solution)/shard_map/all_gather | solution.py:51
  30.0 254.4 %reduce-scatter.3.cloned.1.call-start = ((), (), s32[]{:S(2)}) async-start(), calls=%async_computation.4 | async-start | bytes 8650752 | tf_op jit(solution)/shard_map/reduce_scatter | solution.py:115
  88.5 4.2 %copy-start.2 = (bf16[2048,512]{1,0:T(8,128)(2,1)S(1)}, bf16[2048,512]{1,0:T(8,128)(2,1)}, u32[]{:S(2)}) copy-start(bf16[2048,512]{1,0:T(8,128)(2,1)} %param.9) | copy-start | bytes 6291460
  88.5 4.2 %copy-start.8 = (bf16[512,4096]{1,0:T(8,128)(2,1)S(1)}, bf16[512,4096]{1,0:T(8,128)(2,1)}, u32[]{:S(2)}) copy-start(bf16[512,4096]{1,0:T(8,128)(2,1)} %all-gather.2.cloned.1.call-done) | copy-start | bytes 12582916
  91.5 2.5 copy-start.1
  92.5 2.7 copy-start.4
  92.5 9.4 %collective-permute-start.1 = (f32[256,512]{1,0:T(8,128)}, f32[256,512]{1,0:T(8,128)}, u32[]{:S(2)}, u32[]{:S(2)}) collective-permute-start(f32[256,512]{1,0:T(8,128)} %slice_select_fusion), channel_id=1, source_target_pairs={{0,8},{8,0},{16,24},{24,16},{32,40},{40,32},{48,56},{56,48},{64,72... | collective-permute-start | bytes 1572872 | tf_op jit(solution)/shard_map/ppermute | solution.py:30
  94.0 7.7 %copy-start.9 = (s32[4]{0:T(128)S(1)}, s32[4]{0:T(128)}, u32[]{:S(2)}) copy-start(s32[4]{0:T(128)} %param.11) | copy-start | bytes 52
  94.9 13.3 %collective-permute-start = (f32[256,512]{1,0:T(8,128)}, f32[256,512]{1,0:T(8,128)}, u32[]{:S(2)}, u32[]{:S(2)}) collective-permute-start(f32[256,512]{1,0:T(8,128)} %slice_select_fusion.1), channel_id=1, source_target_pairs={{0,8},{8,0},{16,24},{24,16},{32,40},{40,32},{48,56},{56,48},{64,72... | collective-permute-start | bytes 1572872 | tf_op jit(solution)/shard_map/ppermute | solution.py:30
  101.7 13.3 %copy-start.3 = (bf16[2,128,8,64]{1,3,2,0:T(8,128)(2,1)}, bf16[2,128,8,64]{1,3,2,0:T(8,128)(2,1)S(1)}, u32[]{:S(2)}) copy-start(bf16[2,128,8,64]{1,3,2,0:T(8,128)(2,1)S(1)} %copy.57) | copy-start | bytes 786436
  110.0 5.0 %copy-start.5 = (bf16[2,128,8,64]{1,3,2,0:T(8,128)(2,1)S(1)}, bf16[2,128,8,64]{1,3,2,0:T(8,128)(2,1)}, u32[]{:S(2)}) copy-start(bf16[2,128,8,64]{1,3,2,0:T(8,128)(2,1)} %copy.50) | copy-start | bytes 786436
  110.0 5.0 %copy-start.6 = (bf16[2,128,8,64]{1,3,2,0:T(8,128)(2,1)S(1)}, bf16[2,128,8,64]{1,3,2,0:T(8,128)(2,1)}, u32[]{:S(2)}) copy-start(bf16[2,128,8,64]{1,3,2,0:T(8,128)(2,1)} %copy.49) | copy-start | bytes 786436
  116.1 6.5 %collective-permute-start.3 = (bf16[256,512]{0,1:T(8,128)(2,1)S(1)}, bf16[256,512]{0,1:T(8,128)(2,1)}, u32[]{:S(2)}, u32[]{:S(2)}) collective-permute-start(bf16[256,512]{0,1:T(8,128)(2,1)S(1)} %bitcast.65), channel_id=1, source_target_pairs={{0,8},{8,0},{16,24},{24,16},{32,40},{40,32},{48,56},{56,48},{64,72... | collective-permute-start | bytes 786440 | tf_op jit(solution)/shard_map/ppermute | solution.py:30
  122.1 3.6 collective-permute-start.2
  133.3 151.1 %copy-start.7 = (bf16[2,128,8,64]{1,3,2,0:T(8,128)(2,1)S(1)}, bf16[2,128,8,64]{1,3,2,0:T(8,128)(2,1)}, u32[]{:S(2)}) copy-start(bf16[2,128,8,64]{1,3,2,0:T(8,128)(2,1)} %copy.49) | copy-start | bytes 786436
  133.3 240.5 %reduce-scatter.5.cloned.1.call-start = ((), (), s32[]{:S(2)}) async-start(), calls=%async_computation.5 | async-start | bytes 294912 | tf_op jit(solution)/shard_map/reduce_scatter | solution.py:121
Sparse Core Ops, SparseCore 0:
  30.1 58.3 all-gather.1
  133.5 150.8 reduce-scatter.2
  288.8 84.9 reduce-scatter.4
